TPU v7x, 128 devices: a whole 4x4x4 slice. The times are simulated.
128 devices in a mesh: rep: 4 (over z_lo, core), shard: 32 (over z_hi, y, x).
Axes of the slice: x: 4, y: 4, z: 4 (z_hi: 2, z_lo: 2; z = z_hi * 2 + z_lo), core: 2. Of those that a mesh axis runs over, the one named last changes fastest.
Arguments:
- inputs: float32 [32, 512, 1024], P('shard', 'rep'), may hold values from -6 to 6
- segment_ids: int32 [32, 512], P('shard', 'rep'), may hold values from 0 to 3, never falling along the last dimension, each value on 1 to 200 neighbouring positions
- cotangent: float32 [32, 512, 1024], P('shard', 'rep'), may hold values from -6 to 6
- w_qkv: bfloat16 [1, 1024, 3072], P(None, 'shard'), may hold values from -0.1875 to 0.1875
- w_out: bfloat16 [1, 1024, 1024], P(None, 'shard'), may hold values from -0.75 to 0.75
- w_up: bfloat16 [1, 1024, 4096], P(None, 'shard'), may hold values from -0.1875 to 0.1875
- w_down: bfloat16 [1, 4096, 1024], P(None, 'shard'), may hold values from -0.09375 to 0.09375
- biases: bfloat16 [1, 6, 1024], P(None, None, 'shard'), may hold values from -3 to 3
- norm_gains: bfloat16 [1, 2, 1024], P(None, None, 'shard'), may hold values from 0.5 to 1.5
- up_bias: bfloat16 [1, 4096], P(None, 'shard'), may hold values from -3 to 3
Outputs:
- outputs: float32 [32, 512, 1024], P('shard', 'rep')
- input_grad: float32 [32, 512, 1024], P('shard', 'rep')
- grad_w_qkv: float32 [1, 1024, 3072], P(None, 'shard')
- grad_w_out: float32 [1, 1024, 1024], P(None, 'shard')
- grad_w_up: float32 [1, 1024, 4096], P(None, 'shard')
- grad_w_down: float32 [1, 4096, 1024], P(None, 'shard')
- grad_biases: float32 [1, 6, 1024], P(None, None, 'shard')
- grad_norm_gains: float32 [1, 2, 1024], P(None, None, 'shard')
- grad_up_bias: float32 [1, 4096], P(None, 'shard')
Inputs may be any that keep to these rules, and one draw needn't show every extreme that they name: `segment_ids`: within each sequence the id never falls along the positions; ids of different sequences are unrelated.
All inputs are finite; a program needn't handle non-finite values.
Results may differ from a plain program's by a relative error of at most 0.025.
Values may be sent and summed in bfloat16 or wider, within the bound.
A program may use at most 128 MiB of HBM per device.

v0:
```python
import math
import jax
import jax.numpy as jnp
from jax import lax
from jax.sharding import PartitionSpec as P

D = 1024
HEADS = 16
HEAD_DIM = 64
LAYERS = 1
epsilon = 1e-06


def normalize(residual):
    center = residual - jnp.mean(residual, axis=-1, keepdims=True)
    rstd_val = lax.rsqrt(jnp.mean(center * center, axis=-1, keepdims=True) + epsilon)
    return (center * rstd_val, rstd_val)


def norm_back(grad_out, x_hat, rstd_val, gain_row):
    d_hat = grad_out * gain_row
    return rstd_val * (
        d_hat
        - jnp.mean(d_hat, axis=-1, keepdims=True)
        - x_hat * jnp.mean(d_hat * x_hat, axis=-1, keepdims=True)
    )


def gelu_pair(pre_act):
    normal_cdf = 0.5 * (1.0 + lax.erf(pre_act * (1.0 / math.sqrt(2.0))))
    density = jnp.exp(-0.5 * pre_act * pre_act) * (1.0 / math.sqrt(2.0 * math.pi))
    return (pre_act * normal_cdf, normal_cdf + pre_act * density)


def matmul(first_op, second_op):
    return jnp.dot(first_op, second_op, preferred_element_type=jnp.float32)


def matmul_lt(first_op, second_op):
    return lax.dot_general(
        first_op, second_op, (((0,), (0,)), ((), ())), preferred_element_type=jnp.float32
    )


def matmul_rt(first_op, second_op):
    return lax.dot_general(
        first_op, second_op, (((1,), (1,)), ((), ())), preferred_element_type=jnp.float32
    )


def attention_scores(queries, keys_all, seg_rows, seg_cols):
    scores = jnp.einsum(
        "sqhe,skhe->shqk", queries, keys_all, preferred_element_type=jnp.float32
    ) * (1.0 / math.sqrt(HEAD_DIM))
    allowed = seg_rows[:, None, :, None] == seg_cols[:, None, None, :]
    return (scores, allowed)


def pick(tensor, index, axis):
    return lax.dynamic_index_in_dim(tensor, index, axis=axis, keepdims=False)


def pack_cols(tensor, parts):
    rows = tensor.shape[0]
    return tensor.reshape(rows, parts, -1).transpose(1, 0, 2).reshape(parts, -1)


def unpack_cols(flat, parts, rows):
    return flat.reshape(parts, rows, -1).transpose(1, 0, 2).reshape(rows, -1)


def gather_rep(tensor):
    return lax.all_gather(tensor, "rep", axis=0, tiled=True)


def scatter_rep(tensor):
    return lax.psum_scatter(tensor, "rep", scatter_dimension=0, tiled=True)


def local(inputs, segment_ids, cotangent, w_qkv, w_out, w_up, w_down, biases, norm_gains, up_bias):
    parts = lax.axis_size("shard")
    reps = lax.axis_size("rep")
    r = lax.axis_index("rep")
    head_cols = D // reps
    heads_here = HEADS // reps
    ff_all = w_up.shape[2]
    ff_chunk = ff_all // parts
    ff_piece = ff_chunk // reps
    k_rows = D // parts
    qkv_piece = pick(w_qkv[0].reshape(k_rows, 3, reps, head_cols), r, 2).reshape(k_rows, -1)
    out_piece = w_out[0]
    up_piece = pick(w_up[0].reshape(k_rows, parts, reps, ff_piece), r, 2).reshape(k_rows, -1)
    down_piece = pick(w_down[0].reshape(reps, ff_piece, D), r, 0)
    upb_piece = pick(up_bias[0].reshape(reps, ff_piece), r, 0)
    pieces = (qkv_piece, out_piece, up_piece, down_piece, upb_piece, biases[0], norm_gains[0])
    sizes = [piece.size for piece in pieces]
    offsets = [sum(sizes[:i]) for i in range(len(sizes) + 1)]
    packed = jnp.concatenate([piece.reshape(-1) for piece in pieces])
    packed = jnp.pad(packed, (0, -(-packed.size // 1024) * 1024 - packed.size))
    gathered = lax.all_gather(packed, "shard", axis=0, tiled=False)
    got = [gathered[:, offsets[i] : offsets[i + 1]] for i in range(len(sizes))]
    w_qkv_r = got[0].reshape(D, 3 * head_cols)
    w_out_all = got[1].reshape(D, D)
    w_out_r = lax.dynamic_slice_in_dim(w_out_all, r * head_cols, head_cols, axis=0)
    w_up_r = got[2].reshape(D, -1)
    w_down_r = got[3].reshape(-1, D)
    up_bias_r = got[4].reshape(-1)
    bias_all = unpack_cols(got[5], parts, biases.shape[1])
    gain_all = unpack_cols(got[6], parts, norm_gains.shape[1])
    bias_q = lax.dynamic_slice_in_dim(bias_all[0], r * head_cols, head_cols)
    bias_v = lax.dynamic_slice_in_dim(bias_all[1], r * head_cols, head_cols)
    rows_f32 = inputs[0]
    own = rows_f32.shape[0]
    rows_bf = rows_f32.astype(jnp.bfloat16)
    seg_tag = jnp.broadcast_to(segment_ids[0].astype(jnp.bfloat16)[:, None], (own, 128))
    hb_seg = gather_rep(jnp.concatenate([rows_bf, seg_tag], axis=1))
    hb_all = hb_seg[:, :D]
    seg_all = hb_seg[:, D]
    qkv_rows = matmul(hb_all, w_qkv_r)
    queries = (
        (qkv_rows[:, :head_cols] + bias_q).astype(jnp.bfloat16).reshape(1, -1, heads_here, HEAD_DIM)
    )
    keys_all = (
        qkv_rows[:, head_cols : 2 * head_cols]
        .astype(jnp.bfloat16)
        .reshape(1, -1, heads_here, HEAD_DIM)
    )
    values_all = (
        (qkv_rows[:, 2 * head_cols :] + bias_v)
        .astype(jnp.bfloat16)
        .reshape(1, -1, heads_here, HEAD_DIM)
    )
    seg_rows = seg_all[None]
    scores, allowed = attention_scores(queries, keys_all, seg_rows, seg_rows)
    expo_all = jnp.where(allowed, jnp.exp(scores), 0.0)
    row_total = jnp.sum(expo_all, axis=-1, keepdims=True)
    log_total = jnp.log(row_total)
    attn_probs = (expo_all / row_total).astype(jnp.bfloat16)
    context = (
        jnp.einsum("shqk,skhe->sqhe", attn_probs, values_all, preferred_element_type=jnp.float32)
        .astype(jnp.bfloat16)
        .reshape(-1, head_cols)
    )
    first_sum = rows_f32 + scatter_rep(matmul(context, w_out_r)) + bias_all[2]
    norm_one, rstd_one = normalize(first_sum)
    mid_norm = norm_one * gain_all[0] + bias_all[3]
    mid_b = mid_norm.astype(jnp.bfloat16)
    mid_all = gather_rep(mid_b)
    pre_act = matmul(mid_all, w_up_r) + up_bias_r
    act_f32, gelu_slope = gelu_pair(pre_act)
    act_b = act_f32.astype(jnp.bfloat16)
    second_sum = mid_norm + scatter_rep(matmul(act_b, w_down_r)) + bias_all[4]
    norm_two, rstd_two = normalize(second_sum)
    layer_out = norm_two * gain_all[1] + bias_all[5]
    grad_rows = cotangent[0]
    d_gain_two = jnp.sum(grad_rows * norm_two, axis=0)
    d_bias_two = jnp.sum(grad_rows, axis=0)
    d_second = norm_back(grad_rows, norm_two, rstd_two, gain_all[1])
    d_bdown = jnp.sum(d_second, axis=0)
    d_second_all = gather_rep(d_second.astype(jnp.bfloat16))
    d_wdown = matmul_lt(act_b, d_second_all)
    d_pre = matmul_rt(d_second_all, w_down_r) * gelu_slope
    d_bup = jnp.sum(d_pre, axis=0)
    d_pre_b = d_pre.astype(jnp.bfloat16)
    d_wup = matmul_lt(mid_all, d_pre_b)
    ffn_pack = jnp.concatenate(
        [
            d_wup.astype(jnp.bfloat16).reshape(parts, -1),
            d_wdown.astype(jnp.bfloat16).reshape(parts, -1),
        ],
        axis=1,
    ).reshape(parts, 8, -1)
    ffn_recv = lax.all_to_all(ffn_pack, "shard", 0, 0, tiled=True)
    ffn_share = jnp.sum(ffn_recv.astype(jnp.float32), axis=0).astype(jnp.bfloat16)
    d_mid = d_second + scatter_rep(matmul_rt(d_pre_b, w_up_r))
    d_gain_one = jnp.sum(d_mid * norm_one, axis=0)
    d_bias_one = jnp.sum(d_mid, axis=0)
    d_first = norm_back(d_mid, norm_one, rstd_one, gain_all[0])
    d_bout = jnp.sum(d_first, axis=0)
    d_first_all = gather_rep(d_first.astype(jnp.bfloat16))
    d_wout = matmul_lt(context, d_first_all)
    d_context = (
        matmul_rt(d_first_all, w_out_r).astype(jnp.bfloat16).reshape(1, -1, heads_here, HEAD_DIM)
    )
    probs_again = jnp.where(allowed, jnp.exp(scores - log_total), 0.0)
    d_probs = jnp.einsum(
        "sqhe,skhe->shqk", d_context, values_all, preferred_element_type=jnp.float32
    )
    d_scores = (
        probs_again
        * (d_probs - jnp.sum(probs_again * d_probs, axis=-1, keepdims=True))
        * (1.0 / math.sqrt(HEAD_DIM))
    ).astype(jnp.bfloat16)
    d_queries = jnp.einsum(
        "shqk,skhe->sqhe", d_scores, keys_all, preferred_element_type=jnp.float32
    ).reshape(-1, head_cols)
    d_keys = jnp.einsum(
        "shqk,sqhe->skhe", d_scores, queries, preferred_element_type=jnp.float32
    ).reshape(-1, head_cols)
    d_values = jnp.einsum(
        "shqk,sqhe->skhe",
        probs_again.astype(jnp.bfloat16),
        d_context,
        preferred_element_type=jnp.float32,
    ).reshape(-1, head_cols)
    d_qkv = jnp.concatenate([d_queries, d_keys, d_values], axis=-1).astype(jnp.bfloat16)
    d_wqkv = matmul_lt(hb_all, d_qkv)
    input_grad = d_first + scatter_rep(matmul_rt(d_qkv, w_qkv_r))
    zeros_cols = jnp.zeros((D,), jnp.float32)
    d_bq = lax.dynamic_update_slice_in_dim(zeros_cols, jnp.sum(d_queries, axis=0), r * head_cols, 0)
    d_bv = lax.dynamic_update_slice_in_dim(zeros_cols, jnp.sum(d_values, axis=0), r * head_cols, 0)
    d_biases = jnp.stack([d_bq, d_bv, d_bout, d_bias_one, d_bdown, d_bias_two])
    d_gains = jnp.stack([d_gain_one, d_gain_two])
    d_wout_all = lax.dynamic_update_slice_in_dim(
        jnp.zeros((D, D), jnp.bfloat16), d_wout.astype(jnp.bfloat16), r * head_cols, 0
    )
    d_bup_all = lax.dynamic_update_slice_in_dim(
        jnp.zeros((parts, reps, ff_piece), jnp.float32), d_bup.reshape(parts, 1, ff_piece), r, 1
    )
    grad_parts = (
        d_wqkv.astype(jnp.bfloat16).reshape(parts, -1),
        d_wout_all.reshape(parts, -1),
        d_bup_all.astype(jnp.bfloat16).reshape(parts, -1),
        pack_cols(d_biases.astype(jnp.bfloat16), parts),
        pack_cols(d_gains.astype(jnp.bfloat16), parts),
    )
    g_sizes = [piece.shape[1] for piece in grad_parts]
    grad_pack = jnp.concatenate(grad_parts, axis=1)
    width = grad_pack.shape[1]
    padded = -(-width // 1024) * 1024
    grad_pack = jnp.pad(grad_pack, ((0, 0), (0, padded - width))).reshape(parts, 8, -1)
    received = lax.all_to_all(grad_pack, "shard", 0, 0, tiled=True)
    shares = jnp.sum(received.astype(jnp.float32), axis=0).astype(jnp.bfloat16)
    all_shares = jnp.concatenate([shares.reshape(-1), ffn_share.reshape(-1)])
    joined = lax.all_gather(all_shares, "rep", axis=0, tiled=False).astype(jnp.float32)
    g_sizes = g_sizes + [padded - width, ffn_share.size // 2, ffn_share.size // 2]
    names = ["qkv", "out", "bup", "bias", "gain", "pad", "up", "down"]
    g_offsets = [sum(g_sizes[:i]) for i in range(len(g_sizes) + 1)]
    got = {names[i]: joined[:, g_offsets[i] : g_offsets[i + 1]] for i in range(len(g_sizes))}
    grad_w_qkv = (
        got["qkv"].reshape(reps, k_rows, 3, head_cols).transpose(1, 2, 0, 3).reshape(k_rows, -1)
    )
    grad_w_out = jnp.sum(got["out"], axis=0).reshape(k_rows, D)
    grad_w_up = (
        got["up"].reshape(reps, k_rows, parts, ff_piece).transpose(1, 2, 0, 3).reshape(k_rows, -1)
    )
    grad_w_down = got["down"].reshape(reps * ff_piece, D)
    grad_up_bias = jnp.sum(got["bup"], axis=0)
    grad_biases = jnp.sum(got["bias"], axis=0).reshape(biases.shape[1], -1)
    grad_gains = jnp.sum(got["gain"], axis=0).reshape(norm_gains.shape[1], -1)
    return (
        layer_out[None],
        input_grad[None],
        grad_w_qkv[None],
        grad_w_out[None],
        grad_w_up[None],
        grad_w_down[None],
        grad_biases[None],
        grad_gains[None],
        grad_up_bias[None],
    )


def solution(mesh):
    in_specs = (
        P("shard", "rep", None),
        P("shard", "rep"),
        P("shard", "rep", None),
        P(None, "shard", None),
        P(None, "shard", None),
        P(None, "shard", None),
        P(None, "shard", None),
        P(None, None, "shard"),
        P(None, None, "shard"),
        P(None, "shard"),
    )
    out_specs = (
        P("shard", "rep", None),
        P("shard", "rep", None),
        P(None, "shard", None),
        P(None, "shard", None),
        P(None, "shard", None),
        P(None, "shard", None),
        P(None, None, "shard"),
        P(None, None, "shard"),
        P(None, "shard"),
    )
    return jax.shard_map(local, mesh=mesh, in_specs=in_specs, out_specs=out_specs, check_vma=False)
```

profile of v0, /device:TPU:1, one launch (start us, length us, event | category | flops | bytes accessed | tf_op | source)
XLA Modules:
  0.0 512.8 jit_solution(16374503692966600030)
XLA Ops:
  8.0 1.1 bitcast_convert_fusion
  10.0 1.1 reshape_squeeze.21
  12.3 1.7 dynamic-slice_reduce_fusion
  17.1 18.4 %all-gather.8.cloned.1.call-done = bf16[512,1152]{1,0:T(8,128)(2,1)} async-done(((bf16[128,1152]{1,0:T(8,128)(2,1)}), bf16[512,1152]{1,0:T(8,128)(2,1)}) %all-gather.8.cloned.1.call-update) | async-done | bytes 1179664 | tf_op jit(solution)/shard_map/all_gather | solution.py:73
  37.5 104.4 %all-gather.16.cloned.1.call-done = bf16[3964928]{0:T(1024)(128)(2,1)} async-done(((bf16[123904]{0:T(1024)(128)(2,1)}), bf16[3964928]{0:T(1024)(128)(2,1)}) %all-gather.16.cloned.1.call-update) | async-done | bytes 7929872 | tf_op jit(solution)/shard_map/all_gather | solution.py:100
  141.9 8.3 %reshape.394 = bf16[32,123904]{1,0:T(8,128)(2,1)} reshape(bf16[3964928]{0:T(1024)(128)(2,1)} %all-gather.16.cloned.1.call-done) | data formatting | bytes 15859712 | tf_op jit(solution)/shard_map/all_gather | solution.py:100
  151.1 5.7 %fusion.76 = (bf16[32,32768]{1,0:T(8,128)(2,1)}, bf16[32,32768]{1,0:T(8,128)(2,1)}, bf16[32,32768]{1,0:T(8,128)(2,1)}) fusion(bf16[32,123904]{1,0:T(8,128)(2,1)} %reshape.394), kind=kLoop, calls=%fused_computation.142 | loop fusion | bytes 12582912 | tf_op jit(solution)/shard_map/slice | solution.py:101
  158.8 2.2 fusion.33
  162.8 2.4 reshape.368
  165.1 1.3 fusion.2
  166.5 1.2 fusion.28
  168.5 3.0 fusion.45
  172.9 25.4 %reduce-scatter.5.cloned.1.call-done = f32[128,1024]{1,0:T(8,128)} async-done(((f32[512,1024]{1,0:T(8,128)}), f32[128,1024]{1,0:T(8,128)}) %reduce-scatter.5.cloned.1.call-update) | async-done | bytes 524304 | tf_op jit(solution)/shard_map/reduce_scatter | solution.py:77
  198.3 1.2 fusion.74
  201.9 4.3 reshape.370
  206.3 2.4 reshape.371
  208.6 14.1 %all-gather.10.cloned.1.call-done = bf16[512,1024]{1,0:T(8,128)(2,1)} async-done(((bf16[128,1024]{1,0:T(8,128)(2,1)}), bf16[512,1024]{1,0:T(8,128)(2,1)}) %all-gather.10.cloned.1.call-update) | async-done | bytes 1048592 | tf_op jit(solution)/shard_map/all_gather | solution.py:73
  222.7 4.6 multiply_convert_fusion.1
  228.2 2.6 fusion.83
  231.1 29.0 %reduce-scatter.7.cloned.1.call-done = f32[128,1024]{1,0:T(8,128)} async-done(((f32[512,1024]{1,0:T(8,128)}), f32[128,1024]{1,0:T(8,128)}) %reduce-scatter.7.cloned.1.call-update) | async-done | bytes 524304 | tf_op jit(solution)/shard_map/reduce_scatter | solution.py:77
  260.1 1.3 fusion.73
  261.9 1.0 fusion.71
  263.8 22.0 %all-gather.12.cloned.1.call-done = bf16[512,1024]{1,0:T(8,128)(2,1)} async-done(((bf16[128,1024]{1,0:T(8,128)(2,1)}), bf16[512,1024]{1,0:T(8,128)(2,1)}) %all-gather.12.cloned.1.call-update) | async-done | bytes 1048592 | tf_op jit(solution)/shard_map/all_gather | solution.py:73
  285.7 4.6 fusion.82
  290.4 2.7 fusion.40
  293.4 28.9 %reduce-scatter.9.cloned.1.call-done = f32[128,1024]{1,0:T(8,128)} async-done(((f32[512,1024]{1,0:T(8,128)}), f32[128,1024]{1,0:T(8,128)}) %reduce-scatter.9.cloned.1.call-update) | async-done | bytes 524304 | tf_op jit(solution)/shard_map/reduce_scatter | solution.py:77
  322.3 1.3 multiply_reduce_fusion.1
  324.7 4.2 convolution_convert_fusion
  328.9 3.3 concatenate.33
  332.2 4.2 convolution_convert_fusion.1
  336.5 4.5 concatenate.32
  341.0 4.6 pad_maximum_fusion
  345.6 9.2 %all-to-all-start.1 = ((bf16[32,8,8192]{2,1,0:T(8,128)(2,1)}), bf16[32,8,8192]{2,1,0:T(8,128)(2,1)}, u32[]{:S(2)}, u32[]{:S(2)}) async-start(bf16[32,8,8192]{2,1,0:T(8,128)(2,1)} %pad_maximum_fusion), calls=%async_computation.5 | async-start | bytes 8388608 | tf_op jit(solution)/shard_map/all_to_all | solution.py:173
  355.6 1.8 convolution_convert_fusion.4
  357.5 2.7 fusion.84
  360.8 1.1 fusion.78
  362.0 7.4 %fusion.29 = bf16[4,64,512]{2,1,0:T(8,128)(2,1)S(1)} fusion(bf16[512,4,64]{0,2,1:T(8,128)(2,1)S(1)} %bitcast.116, f32[4,512,512]{1,2,0:T(8,128)} %fusion.84, f32[4,512,512]{1,2,0:T(8,128)} %copy-done.30, f32[4,512]{1,0:T(4,128)S(1)} %log.8, pred[512,512]{0,1:T(8,128)(4,1)S(1)} %copy-done.14), kind=kOutput, calls=%fused_computation.33 | convolution fusion | flops 145885696 | bytes 9183232 | tf_op jit(solution)/shard_map/shqk,sqhe->skhe/dot_general | solution.py:197
  369.5 8.8 %fusion.79 = (bf16[4,64]{1,0:T(4,128)(2,1)S(1)}, bf16[1,512,4,64]{1,3,2,0:T(8,128)(2,1)S(1)}) fusion(bf16[512,4,64]{0,2,1:T(8,128)(2,1)S(1)} %bitcast.114, f32[4,512,512]{1,2,0:T(8,128)} %fusion.84, f32[4,512]{1,0:T(4,128)S(1)} %log.8, f32[4,512,512]{1,2,0:T(8,128)} %copy-done.30, pred[512,512]{0,1:T(8,128)(4,1)S(1)} %copy-done.14), kind=kOutput, calls=%fused_computation.145 | convolution fusion | flops 146016512 | bytes 9183744 | tf_op jit(solution)/shard_map/shqk,skhe->sqhe/dot_general | solution.py:194
  378.3 2.2 convolution_convert_fusion.2
  380.5 1.9 reshape.376
  382.4 1.2 constant_dynamic-update-slice_fusion.8
  383.6 1.7 broadcast_in_dim.35
  385.3 1.3 fusion.21
  386.6 2.9 reshape.377
  390.1 1.5 constant_dynamic-update-slice_fusion.7
  392.2 1.3 dynamic-update-slice.3
  393.5 1.4 dynamic-update-slice.4
  394.9 2.3 pad.9
  397.2 2.2 copy.76
  399.4 9.7 %all-to-all-done.1 = bf16[32,8,8192]{2,1,0:T(8,128)(2,1)} async-done(((bf16[32,8,8192]{2,1,0:T(8,128)(2,1)}), bf16[32,8,8192]{2,1,0:T(8,128)(2,1)}, u32[]{:S(2)}, u32[]{:S(2)}) %all-to-all-start.1) | async-done | bytes 4194336 | tf_op jit(solution)/shard_map/all_to_all | solution.py:173
  409.2 7.0 %all-to-all-start = ((bf16[32,8,7296]{2,1,0:T(8,128)(2,1)}), bf16[32,8,7296]{2,1,0:T(8,128)(2,1)}, u32[]{:S(2)}, u32[]{:S(2)}) async-start(bf16[32,8,7296]{2,1,0:T(8,128)(2,1)} %bitcast.97), calls=%async_computation.4 | async-start | bytes 7471104 | tf_op jit(solution)/shard_map/all_to_all | solution.py:232
  416.5 2.5 fusion.47
  418.9 2.8 reduce_sum.251
  421.8 39.6 %all-to-all-done = bf16[32,8,7296]{2,1,0:T(8,128)(2,1)} async-done(((bf16[32,8,7296]{2,1,0:T(8,128)(2,1)}), bf16[32,8,7296]{2,1,0:T(8,128)(2,1)}, u32[]{:S(2)}, u32[]{:S(2)}) %all-to-all-start) | async-done | bytes 3735584 | tf_op jit(solution)/shard_map/all_to_all | solution.py:232
  461.4 2.6 reduce_sum.250
  464.2 17.7 %all-gather.1 = bf16[495616]{0:T(1024)(128)(2,1)} all-gather(bf16[123904]{0:T(1024)(128)(2,1)S(1)} %pad_maximum_fusion.5), channel_id=3, replica_groups=mesh['rep'=4,'shard'=32] {'rep'}, dimensions={0}, use_global_device_ids=true | all-gather | bytes 1239040 | tf_op jit(solution)/shard_map/all_gather | solution.py:235
  481.8 2.1 reshape.396
  484.8 1.3 reshape.385
  487.1 1.9 broadcast_in_dim_reshape.18
  491.4 3.1 copy.79
  494.5 4.5 broadcast_in_dim_reshape.20
  499.0 1.2 broadcast_in_dim_reshape.21
  502.9 1.2 slice_reduce_fusion.5
  504.1 1.9 add_bitcast_fusion
  (194 shorter events, 30.9 us)
Async XLA Ops:
  7.2 7.0 %copy-start = (bf16[1,128,1024]{2,1,0:T(8,128)(2,1)S(1)}, bf16[1,128,1024]{2,1,0:T(8,128)(2,1)}, u32[]{:S(2)}) copy-start(bf16[1,128,1024]{2,1,0:T(8,128)(2,1)} %param.16) | copy-start | bytes 786436
  7.2 4.2 copy-start.19
  7.2 4.3 copy-start.13
  7.2 28.4 %all-gather.8.cloned.1.call-start = ((), (), s32[]{:S(2)}) async-start(), calls=%async_computation.6 | async-start | bytes 1474560 | tf_op jit(solution)/shard_map/all_gather | solution.py:73
  9.1 5.6 %copy-start.22 = (bf16[1,128]{1,0:T(2,128)(2,1)S(1)}, bf16[1,128]{1,0:T(2,128)(2,1)}, u32[]{:S(2)}) copy-start(bf16[1,128]{1,0:T(2,128)(2,1)} %param.19) | copy-start | bytes 772
  9.1 6.4 %copy-start.21 = (bf16[1,6,32]{2,1,0:T(8,128)(2,1)S(1)}, bf16[1,6,32]{2,1,0:T(8,128)(2,1)}, u32[]{:S(2)}) copy-start(bf16[1,6,32]{2,1,0:T(8,128)(2,1)} %param.17) | copy-start | bytes 1156
  9.2 6.4 %copy-start.23 = (bf16[1,2,32]{2,1,0:T(2,128)(2,1)S(1)}, bf16[1,2,32]{2,1,0:T(2,128)(2,1)}, u32[]{:S(2)}) copy-start(bf16[1,2,32]{2,1,0:T(2,128)(2,1)} %param.18) | copy-start | bytes 388
  9.9 132.0 %all-gather.16.cloned.1.call-start = ((), (), s32[]{:S(2)}) async-start(), calls=%async_computation.14 | async-start | bytes 8177664 | tf_op jit(solution)/shard_map/all_gather | solution.py:100
  17.1 181.2 %reduce-scatter.5.cloned.1.call-start = ((), (), s32[]{:S(2)}) async-start(), calls=%async_computation.7 | async-start | bytes 2621440 | tf_op jit(solution)/shard_map/reduce_scatter | solution.py:77
  151.1 5.8 %slice-start = ((bf16[32,123904]{1,0:T(8,128)(2,1)}), bf16[32,24576]{1,0:T(8,128)(2,1)S(1)}, s32[]{:S(2)}) async-start(bf16[32,123904]{1,0:T(8,128)(2,1)} %reshape.394), calls=%async_computation.15 | async-start | bytes 3145728 | tf_op jit(solution)/shard_map/slice | solution.py:101
  157.7 1.2 copy-start.10
  161.0 1.7 copy-start.3
  161.6 3.6 copy-start.17
  161.7 3.4 copy-start.15
  162.8 2.4 copy-start.14
  166.5 2.0 copy-start.30
  168.5 29.9 %copy-start.8 = (f32[1,128,1024]{2,1,0:T(8,128)S(1)}, f32[1,128,1024]{2,1,0:T(8,128)}, u32[]{:S(2)}) copy-start(f32[1,128,1024]{2,1,0:T(8,128)} %param.10) | copy-start | bytes 1572868
  171.5 51.2 %all-gather.10.cloned.1.call-start = ((), (), s32[]{:S(2)}) async-start(), calls=%async_computation.8 | async-start | bytes 1310720 | tf_op jit(solution)/shard_map/all_gather | solution.py:73
  200.6 59.4 %reduce-scatter.7.cloned.1.call-start = ((), (), s32[]{:S(2)}) async-start(), calls=%async_computation.9 | async-start | bytes 2621440 | tf_op jit(solution)/shard_map/reduce_scatter | solution.py:77
  201.9 4.3 copy-start.2
  208.6 19.6 %copy-start.7 = (bf16[1024,1024]{1,0:T(8,128)(2,1)S(1)}, bf16[1024,1024]{1,0:T(8,128)(2,1)}, u32[]{:S(2)}) copy-start(bf16[1024,1024]{1,0:T(8,128)(2,1)} %reshape.371) | copy-start | bytes 6291460
  227.3 1.0 copy-start.32
  230.8 30.8 %copy-start.5 = (f32[1,128,1024]{2,1,0:T(8,128)S(1)}, f32[1,128,1024]{2,1,0:T(8,128)}, u32[]{:S(2)}) copy-start(f32[1,128,1024]{2,1,0:T(8,128)} %param.12) | copy-start | bytes 1572868
  230.8 54.9 %all-gather.12.cloned.1.call-start = ((), (), s32[]{:S(2)}) async-start(), calls=%async_computation.10 | async-start | bytes 1310720 | tf_op jit(solution)/shard_map/all_gather | solution.py:73
  263.7 58.6 %reduce-scatter.9.cloned.1.call-start = ((), (), s32[]{:S(2)}) async-start(), calls=%async_computation.11 | async-start | bytes 2621440 | tf_op jit(solution)/shard_map/reduce_scatter | solution.py:77
  285.7 4.6 copy-start.6
  290.3 2.7 copy-start.33
  293.1 62.5 %all-gather.14.cloned.1.call-start = ((), (), s32[]{:S(2)}) async-start(), calls=%async_computation.12 | async-start | bytes 1310720 | tf_op jit(solution)/shard_map/all_gather | solution.py:73
  345.6 63.6 %all-to-all-start.1 = ((bf16[32,8,8192]{2,1,0:T(8,128)(2,1)}), bf16[32,8,8192]{2,1,0:T(8,128)(2,1)}, u32[]{:S(2)}, u32[]{:S(2)}) async-start(bf16[32,8,8192]{2,1,0:T(8,128)(2,1)} %pad_maximum_fusion), calls=%async_computation.5 | async-start | bytes 8388608 | tf_op jit(solution)/shard_map/all_to_all | solution.py:173
  357.4 3.4 copy-start.31
  360.8 1.1 copy-start.18
  362.0 16.3 %copy-start.24 = (bf16[1,512,4,64]{1,3,2,0:T(8,128)(2,1)}, bf16[1,512,4,64]{1,3,2,0:T(8,128)(2,1)S(1)}, u32[]{:S(2)}) copy-start(bf16[1,512,4,64]{1,3,2,0:T(8,128)(2,1)S(1)} %get-tuple-element.43) | copy-start | bytes 786436
  362.0 7.5 %copy-start.16 = (bf16[512,256]{0,1:T(8,128)(2,1)S(1)}, bf16[512,256]{0,1:T(8,128)(2,1)}, u32[]{:S(2)}) copy-start(bf16[512,256]{0,1:T(8,128)(2,1)} %copy-done.15) | copy-start | bytes 786436
  369.5 8.9 %copy-start.26 = (bf16[4,64,512]{2,1,0:T(8,128)(2,1)}, bf16[4,64,512]{2,1,0:T(8,128)(2,1)S(1)}, u32[]{:S(2)}) copy-start(bf16[4,64,512]{2,1,0:T(8,128)(2,1)S(1)} %fusion.29) | copy-start | bytes 786436
  369.5 8.9 %copy-start.20 = (bf16[512,1152]{1,0:T(8,128)(2,1)S(1)}, bf16[512,1152]{1,0:T(8,128)(2,1)}, u32[]{:S(2)}) copy-start(bf16[512,1152]{1,0:T(8,128)(2,1)} %all-gather.8.cloned.1.call-done) | copy-start | bytes 3538948
  378.3 2.2 copy-start.28
  382.4 2.9 copy-start.12
  409.2 7.3 %copy-start.11 = (bf16[1024,768]{1,0:T(8,128)(2,1)S(1)}, bf16[1024,768]{1,0:T(8,128)(2,1)}, u32[]{:S(2)}) copy-start(bf16[1024,768]{1,0:T(8,128)(2,1)} %copy-done.10) | copy-start | bytes 4718596
  409.2 7.3 %copy-start.25 = (bf16[1,512,4,64]{1,3,2,0:T(8,128)(2,1)S(1)}, bf16[1,512,4,64]{1,3,2,0:T(8,128)(2,1)}, u32[]{:S(2)}) copy-start(bf16[1,512,4,64]{1,3,2,0:T(8,128)(2,1)} %copy-done.24) | copy-start | bytes 786436
  409.2 7.3 %copy-start.27 = (bf16[4,64,512]{2,1,0:T(8,128)(2,1)S(1)}, bf16[4,64,512]{2,1,0:T(8,128)(2,1)}, u32[]{:S(2)}) copy-start(bf16[4,64,512]{2,1,0:T(8,128)(2,1)} %copy-done.26) | copy-start | bytes 786436
  409.2 7.3 %copy-start.29 = (bf16[1,512,4,64]{1,3,2,0:T(8,128)(2,1)S(1)}, bf16[1,512,4,64]{1,3,2,0:T(8,128)(2,1)}, u32[]{:S(2)}) copy-start(bf16[1,512,4,64]{1,3,2,0:T(8,128)(2,1)} %copy-done.28) | copy-start | bytes 786436
  409.2 52.2 %all-to-all-start = ((bf16[32,8,7296]{2,1,0:T(8,128)(2,1)}), bf16[32,8,7296]{2,1,0:T(8,128)(2,1)}, u32[]{:S(2)}, u32[]{:S(2)}) async-start(bf16[32,8,7296]{2,1,0:T(8,128)(2,1)} %bitcast.97), calls=%async_computation.4 | async-start | bytes 7471104 | tf_op jit(solution)/shard_map/all_to_all | solution.py:232
  416.2 87.9 %reduce-scatter.11.cloned.1.call-start = ((), (), s32[]{:S(2)}) async-start(), calls=%async_computation.13 | async-start | bytes 2621440 | tf_op jit(solution)/shard_map/reduce_scatter | solution.py:77
  483.9 6.1 %copy-start.4 = (f32[4,123904]{1,0:T(4,128)}, f32[4,123904]{1,0:T(4,128)S(1)}, u32[]{:S(2)}) copy-start(f32[4,123904]{1,0:T(4,128)S(1)} %reshape.396) | copy-start | bytes 5947396
  494.5 4.5 copy-start.9
  494.5 11.5 %copy-start.1 = (bf16[1,128,1024]{2,1,0:T(8,128)(2,1)S(1)}, bf16[1,128,1024]{2,1,0:T(8,128)(2,1)}, u32[]{:S(2)}) copy-start(bf16[1,128,1024]{2,1,0:T(8,128)(2,1)} %param.16) | copy-start | bytes 786436
Sparse Core Ops, SparseCore 0:
  10.3 25.2 all-gather.7
  39.3 102.5 all-gather.15
  171.6 26.7 reduce-scatter.4
  200.8 21.8 all-gather.9
  231.0 29.0 reduce-scatter.6
  263.8 21.8 all-gather.11
  293.2 29.0 reduce-scatter.8
  324.8 21.8 all-gather.13
  419.5 60.7 reduce-scatter.10
where the time goes:
time: 522 us; the launch traced here: 513 us
  waiting for transfers between devices  292 us (56%)
  local copies, waits for them, and re-layouts  83.9 us (16%)
  matrix products  58.5 us (11%)
  other arithmetic  28.9 us (6%)
  blocking collectives  17.7 us (3%)
  starting transfers between devices  17.3 us (3%)
  between operations  14.8 us (3%)
    all_gather x1, waiting for transfers between devices, local(): gathered = lax.all_gather(packed, 'shard', axis=0, tiled=False)  104 us
    reduce_scatter x4, waiting for transfers between devices, scatter_rep(): return lax.psum_scatter(tensor, 'rep', scatter_dimension=0, tiled=True)  83.3 us
    all_gather x4, waiting for transfers between devices, gather_rep(): return lax.all_gather(tensor, 'rep', axis=0, tiled=True)  54.5 us
    all_to_all x1, waiting for transfers between devices, local(): received = lax.all_to_all(grad_pack, 'shard', 0, 0, tiled=True)  39.6 us
    all_gather x1, blocking collectives, local(): lax.all_gather(all_shares, 'rep', axis=0, tiled=False).astype(jnp.float32)  17.7 us
    dot_general x4, matrix products, matmul(): return jnp.dot(first_op, second_op, preferred_element_type=jnp.float32)  12.3 us
    dot_general x4, matrix products, matmul_lt(): lax.dot_general(first_op, second_op, (((0,), (0,)), ((), ())), preferred_...  12 us
    unnamed x83, local copies, waits for them, and re-layouts  11.9 us
  transfers between devices with their start and end apart: 11, of which 9 were waited for; matrix products, arithmetic and copies ran while one was open for 22% of the time, Pallas kernels for 0%

commit v1 on v0

--- a/solution.py
+++ b/solution.py
@@ -9,6 +9,13 @@
 HEAD_DIM = 64
 LAYERS = 1
 epsilon = 1e-06
+
+
+def gather_over(array, axis, d):
+    peers = lax.axis_size(axis)
+    blocks = jnp.stack([array for _ in range(peers)])
+    blocks = lax.all_to_all(blocks, axis, split_axis=0, concat_axis=0)
+    return jnp.concatenate(blocks, axis=d)
 
 
 def normalize(residual):
@@ -70,7 +77,7 @@
 
 
 def gather_rep(tensor):
-    return lax.all_gather(tensor, "rep", axis=0, tiled=True)
+    return gather_over(tensor, "rep", 0)
 
 
 def scatter_rep(tensor):

time: 522 us -> 493 us (0.944)
  waiting for transfers between devices: 292 us -> 225 us
  blocking collectives: 17.7 us -> 35.4 us
  starting transfers between devices: 17.3 us -> 32.7 us
  local copies, waits for them, and re-layouts: 83.9 us -> 94.4 us
    all_gather x4 -> x0, waiting for transfers between devices: 54.5 us -> none  [gather_rep(): return lax.all_gather(tensor, 'rep', axis=0, tiled=True)]
    all_to_all x0 -> x3, waiting for transfers between devices: none -> 31.6 us  [gather_over(): blocks = lax.all_to_all(blocks, axis, split_axis=0, concat_axis=0)]
    all_gather x1, waiting for transfers between devices: 104 us -> 79.8 us  [local(): gathered = lax.all_gather(packed, 'shard', axis=0, tiled=False)]
    all_to_all x0 -> x1, blocking collectives: none -> 17 us  [gather_over(): blocks = lax.all_to_all(blocks, axis, split_axis=0, concat_axis=0)]
    reduce_scatter x4, waiting for transfers between devices: 83.3 us -> 67.8 us  [scatter_rep(): return lax.psum_scatter(tensor, 'rep', scatter_dimension=0, tiled=True)]
    all_to_all x0 -> x3, starting transfers between devices: none -> 14.1 us  [gather_over(): blocks = lax.all_to_all(blocks, axis, split_axis=0, concat_axis=0)]
    unnamed x83 -> x89, local copies, waits for them, and re-layouts: 11.9 us -> 12.7 us
  transfers between devices with their start and end apart: 11 -> 10, of which waited for: 9 -> 9; matrix products, arithmetic and copies ran while one was open for 22% -> 23% of each run, Pallas kernels for 0% -> 0%
where the time goes in v1:
time: 493 us; the launch traced here: 487 us
  waiting for transfers between devices  225 us (46%)
  local copies, waits for them, and re-layouts  94.4 us (19%)
  matrix products  59.5 us (12%)
  blocking collectives  35.4 us (7%)
  starting transfers between devices  32.7 us (7%)
  other arithmetic  26.2 us (5%)
  between operations  14.7 us (3%)
    all_gather x1, waiting for transfers between devices, local(): gathered = lax.all_gather(packed, 'shard', axis=0, tiled=False)  79.8 us
    reduce_scatter x4, waiting for transfers between devices, scatter_rep(): return lax.psum_scatter(tensor, 'rep', scatter_dimension=0, tiled=True)  67.8 us
    all_to_all x1, waiting for transfers between devices, local(): received = lax.all_to_all(grad_pack, 'shard', 0, 0, tiled=True)  39.4 us
    all_to_all x3, waiting for transfers between devices, gather_over(): blocks = lax.all_to_all(blocks, axis, split_axis=0, concat_axis=0)  31.6 us
    all_gather x1, blocking collectives, local(): lax.all_gather(all_shares, 'rep', axis=0, tiled=False).astype(jnp.float32)  18.4 us
    all_to_all x1, blocking collectives, gather_over(): blocks = lax.all_to_all(blocks, axis, split_axis=0, concat_axis=0)  17 us
    all_to_all x3, starting transfers between devices, gather_over(): blocks = lax.all_to_all(blocks, axis, split_axis=0, concat_axis=0)  14.1 us
    dot_general x4, matrix products, matmul(): return jnp.dot(first_op, second_op, preferred_element_type=jnp.float32)  14 us
  transfers between devices with their start and end apart: 10, of which 9 were waited for; matrix products, arithmetic and copies ran while one was open for 23% of the time, Pallas kernels for 0%

profile of v1, /device:TPU:1, one launch (start us, length us, event | category | flops | bytes accessed | tf_op | source)
XLA Modules:
  0.0 487.4 jit_solution(14878913216126134870)
XLA Ops:
  9.7 1.7 reshape_squeeze.23
  11.4 1.7 dynamic-slice_reduce_fusion
  17.8 4.9 %all-to-all-start = ((bf16[4,128,1152]{1,2,0:T(8,128)(2,1)}), bf16[4,128,1152]{1,2,0:T(8,128)(2,1)S(1)}, u32[]{:S(2)}, u32[]{:S(2)}) async-start(bf16[4,128,1152]{1,2,0:T(8,128)(2,1)} %stack.62), calls=%async_computation | async-start | bytes 2359296 | tf_op jit(solution)/shard_map/all_to_all | solution.py:17
  23.0 16.6 %all-to-all-done = bf16[4,128,1152]{1,2,0:T(8,128)(2,1)S(1)} async-done(((bf16[4,128,1152]{1,2,0:T(8,128)(2,1)}), bf16[4,128,1152]{1,2,0:T(8,128)(2,1)S(1)}, u32[]{:S(2)}, u32[]{:S(2)}) %all-to-all-start) | async-done | bytes 1179680 | tf_op jit(solution)/shard_map/all_to_all | solution.py:17
  39.5 1.4 copy.72
  42.9 79.8 %all-gather.4.cloned.1.call-done = bf16[3964928]{0:T(1024)(128)(2,1)} async-done(((bf16[123904]{0:T(1024)(128)(2,1)}), bf16[3964928]{0:T(1024)(128)(2,1)}) %all-gather.4.cloned.1.call-update) | async-done | bytes 7929872 | tf_op jit(solution)/shard_map/all_gather | solution.py:107
  122.7 8.3 %reshape.418 = bf16[32,123904]{1,0:T(8,128)(2,1)} reshape(bf16[3964928]{0:T(1024)(128)(2,1)} %all-gather.4.cloned.1.call-done) | data formatting | bytes 15859712 | tf_op jit(solution)/shard_map/all_gather | solution.py:107
  131.9 5.8 %fusion.76 = (bf16[32,32768]{1,0:T(8,128)(2,1)}, bf16[32,32768]{1,0:T(8,128)(2,1)}, bf16[32,32768]{1,0:T(8,128)(2,1)}) fusion(bf16[32,123904]{1,0:T(8,128)(2,1)} %reshape.418), kind=kLoop, calls=%fused_computation.142 | loop fusion | bytes 12582912 | tf_op jit(solution)/shard_map/slice | solution.py:108
  137.7 1.6 reshape.383
  139.4 3.9 fusion.33
  144.8 2.0 fusion.35
  148.9 2.4 reshape.389
  151.3 2.3 fusion.2
  153.6 1.2 fusion.28
  156.3 2.8 fusion.45
  160.5 25.4 %reduce-scatter.5.cloned.1.call-done = f32[128,1024]{1,0:T(8,128)} async-done(((f32[512,1024]{1,0:T(8,128)}), f32[128,1024]{1,0:T(8,128)}) %reduce-scatter.5.cloned.1.call-update) | async-done | bytes 524304 | tf_op jit(solution)/shard_map/reduce_scatter | solution.py:84
  188.7 4.6 all-to-all-start.1
  194.1 4.4 reshape.392
  198.4 2.3 reshape.393
  200.7 6.2 %all-to-all-done.1 = bf16[4,128,1024]{2,1,0:T(8,128)(2,1)} async-done(((bf16[4,128,1024]{2,1,0:T(8,128)(2,1)}), bf16[4,128,1024]{2,1,0:T(8,128)(2,1)}, u32[]{:S(2)}, u32[]{:S(2)}) %all-to-all-start.1) | async-done | bytes 1048608 | tf_op jit(solution)/shard_map/all_to_all | solution.py:17
  207.0 4.7 multiply_convert_fusion.1
  211.7 2.6 fusion.83
  214.6 29.6 %reduce-scatter.7.cloned.1.call-done = f32[128,1024]{1,0:T(8,128)} async-done(((f32[512,1024]{1,0:T(8,128)}), f32[128,1024]{1,0:T(8,128)}) %reduce-scatter.7.cloned.1.call-update) | async-done | bytes 524304 | tf_op jit(solution)/shard_map/reduce_scatter | solution.py:84
  244.2 1.3 fusion.73
  247.2 17.0 %all_to_all.30 = bf16[4,128,1024]{2,1,0:T(8,128)(2,1)S(1)} all-to-all(bf16[4,128,1024]{2,1,0:T(8,128)(2,1)S(1)} %stack.64), channel_id=1, replica_groups=mesh['rep'=4,'shard'=32] {'rep'}, dimensions={0} | all-to-all | bytes 2097152 | tf_op jit(solution)/shard_map/all_to_all | solution.py:17
  264.3 2.1 fusion.82
  267.4 2.7 fusion.40
  271.3 3.8 convolution_convert_fusion
  275.2 3.3 concatenate.33
  278.5 4.1 convolution_convert_fusion.1
  282.6 4.5 concatenate.32
  287.4 12.7 %reduce-scatter.9.cloned.1.call-done = f32[128,1024]{1,0:T(8,128)} async-done(((f32[512,1024]{1,0:T(8,128)}), f32[128,1024]{1,0:T(8,128)}) %reduce-scatter.9.cloned.1.call-update) | async-done | bytes 524304 | tf_op jit(solution)/shard_map/reduce_scatter | solution.py:84
  300.2 1.3 multiply_reduce_fusion.1
  302.9 4.6 all-to-all-start.3
  307.5 4.6 pad_maximum_fusion
  312.4 8.8 %all-to-all-done.3 = bf16[4,128,1024]{2,1,0:T(8,128)(2,1)} async-done(((bf16[4,128,1024]{2,1,0:T(8,128)(2,1)}), bf16[4,128,1024]{2,1,0:T(8,128)(2,1)}, u32[]{:S(2)}, u32[]{:S(2)}) %all-to-all-start.3) | async-done | bytes 1048608 | tf_op jit(solution)/shard_map/all_to_all | solution.py:17
  321.2 9.4 %all-to-all-start.5 = ((bf16[32,8,8192]{2,1,0:T(8,128)(2,1)}), bf16[32,8,8192]{2,1,0:T(8,128)(2,1)}, u32[]{:S(2)}, u32[]{:S(2)}) async-start(bf16[32,8,8192]{2,1,0:T(8,128)(2,1)} %pad_maximum_fusion), calls=%async_computation.9 | async-start | bytes 8388608 | tf_op jit(solution)/shard_map/all_to_all | solution.py:180
  330.6 1.9 convolution_convert_fusion.4
  332.5 2.8 fusion.84
  337.3 7.4 %fusion.29 = bf16[4,64,512]{2,1,0:T(8,128)(2,1)S(1)} fusion(bf16[512,4,64]{0,2,1:T(8,128)(2,1)S(1)} %bitcast.125, f32[4,512,512]{1,2,0:T(8,128)} %fusion.84, f32[4,512,512]{1,2,0:T(8,128)} %copy-done.32, f32[4,512]{1,0:T(4,128)S(1)} %log.8, pred[512,512]{0,1:T(8,128)(4,1)S(1)} %copy-done.20), kind=kOutput, calls=%fused_computation.33 | convolution fusion | flops 145885696 | bytes 9183232 | tf_op jit(solution)/shard_map/shqk,sqhe->skhe/dot_general | solution.py:204
  344.7 8.8 %fusion.79 = (bf16[4,64]{1,0:T(4,128)(2,1)S(1)}, bf16[1,512,4,64]{1,3,2,0:T(8,128)(2,1)S(1)}) fusion(bf16[512,4,64]{0,2,1:T(8,128)(2,1)S(1)} %bitcast.123, f32[4,512,512]{1,2,0:T(8,128)} %fusion.84, f32[4,512]{1,0:T(4,128)S(1)} %log.8, f32[4,512,512]{1,2,0:T(8,128)} %copy-done.32, pred[512,512]{0,1:T(8,128)(4,1)S(1)} %copy-done.20), kind=kOutput, calls=%fused_computation.145 | convolution fusion | flops 146016512 | bytes 9183744 | tf_op jit(solution)/shard_map/shqk,skhe->sqhe/dot_general | solution.py:201
  353.6 2.2 convolution_convert_fusion.2
  355.7 1.9 reshape.400
  358.9 1.7 broadcast_in_dim.35
  360.5 2.5 fusion.21
  363.1 2.9 reshape.401
  366.5 1.5 constant_dynamic-update-slice_fusion.7
  368.6 1.3 dynamic-update-slice.3
  370.0 1.4 dynamic-update-slice.4
  371.4 2.3 pad.9
  373.7 2.2 copy.94
  375.9 6.0 %all-to-all-done.5 = bf16[32,8,8192]{2,1,0:T(8,128)(2,1)} async-done(((bf16[32,8,8192]{2,1,0:T(8,128)(2,1)}), bf16[32,8,8192]{2,1,0:T(8,128)(2,1)}, u32[]{:S(2)}, u32[]{:S(2)}) %all-to-all-start.5) | async-done | bytes 4194336 | tf_op jit(solution)/shard_map/all_to_all | solution.py:180
  381.8 8.5 %all-to-all-start.4 = ((bf16[32,8,7296]{2,1,0:T(8,128)(2,1)}), bf16[32,8,7296]{2,1,0:T(8,128)(2,1)}, u32[]{:S(2)}, u32[]{:S(2)}) async-start(bf16[32,8,7296]{2,1,0:T(8,128)(2,1)} %bitcast.101), calls=%async_computation.8 | async-start | bytes 7471104 | tf_op jit(solution)/shard_map/all_to_all | solution.py:239
  390.6 2.5 fusion.47
  393.1 2.8 reduce_sum.251
  395.9 39.4 %all-to-all-done.4 = bf16[32,8,7296]{2,1,0:T(8,128)(2,1)} async-done(((bf16[32,8,7296]{2,1,0:T(8,128)(2,1)}), bf16[32,8,7296]{2,1,0:T(8,128)(2,1)}, u32[]{:S(2)}, u32[]{:S(2)}) %all-to-all-start.4) | async-done | bytes 3735584 | tf_op jit(solution)/shard_map/all_to_all | solution.py:239
  435.3 2.6 reduce_sum.250
  438.1 18.4 %all-gather.1 = bf16[495616]{0:T(1024)(128)(2,1)} all-gather(bf16[123904]{0:T(1024)(128)(2,1)S(1)} %pad_maximum_fusion.5), channel_id=3, replica_groups=mesh['rep'=4,'shard'=32] {'rep'}, dimensions={0}, use_global_device_ids=true | all-gather | bytes 1239040 | tf_op jit(solution)/shard_map/all_gather | solution.py:242
  456.5 2.1 reshape.420
  459.4 1.3 reshape.409
  461.8 1.9 broadcast_in_dim_reshape.18
  466.1 3.1 copy.97
  469.2 4.5 broadcast_in_dim_reshape.20
  478.8 1.9 add_bitcast_fusion
  (201 shorter events, 40.3 us)
Async XLA Ops:
  7.2 6.1 %copy-start = (bf16[1,128,1024]{2,1,0:T(8,128)(2,1)S(1)}, bf16[1,128,1024]{2,1,0:T(8,128)(2,1)}, u32[]{:S(2)}) copy-start(bf16[1,128,1024]{2,1,0:T(8,128)(2,1)} %param.16) | copy-start | bytes 786436
  7.2 6.7 %copy-start.25 = (bf16[1,128]{1,0:T(2,128)(2,1)S(1)}, bf16[1,128]{1,0:T(2,128)(2,1)}, u32[]{:S(2)}) copy-start(bf16[1,128]{1,0:T(2,128)(2,1)} %param.19) | copy-start | bytes 772
  7.2 7.4 %copy-start.24 = (bf16[1,6,32]{2,1,0:T(8,128)(2,1)S(1)}, bf16[1,6,32]{2,1,0:T(8,128)(2,1)}, u32[]{:S(2)}) copy-start(bf16[1,6,32]{2,1,0:T(8,128)(2,1)} %param.17) | copy-start | bytes 1156
  7.2 7.5 %copy-start.26 = (bf16[1,2,32]{2,1,0:T(2,128)(2,1)S(1)}, bf16[1,2,32]{2,1,0:T(2,128)(2,1)}, u32[]{:S(2)}) copy-start(bf16[1,2,32]{2,1,0:T(2,128)(2,1)} %param.18) | copy-start | bytes 388
  7.2 115.5 %all-gather.4.cloned.1.call-start = ((), (), s32[]{:S(2)}) async-start(), calls=%async_computation.14 | async-start | bytes 8177664 | tf_op jit(solution)/shard_map/all_gather | solution.py:107
  8.7 7.5 %copy-start.27 = (s32[1,128]{1,0:T(1,128)S(1)}, s32[1,128]{1,0:T(1,128)}, u32[]{:S(2)}) copy-start(s32[1,128]{1,0:T(1,128)} %param.11) | copy-start | bytes 1540
  8.7 7.5 %copy-start.9 = (f32[1,128,1024]{2,1,0:T(8,128)S(1)}, f32[1,128,1024]{2,1,0:T(8,128)}, u32[]{:S(2)}) copy-start(f32[1,128,1024]{2,1,0:T(8,128)} %param.10) | copy-start | bytes 1572868
  17.8 21.8 %all-to-all-start = ((bf16[4,128,1152]{1,2,0:T(8,128)(2,1)}), bf16[4,128,1152]{1,2,0:T(8,128)(2,1)S(1)}, u32[]{:S(2)}, u32[]{:S(2)}) async-start(bf16[4,128,1152]{1,2,0:T(8,128)(2,1)} %stack.62), calls=%async_computation | async-start | bytes 2359296 | tf_op jit(solution)/shard_map/all_to_all | solution.py:17
  22.7 163.3 %reduce-scatter.5.cloned.1.call-start = ((), (), s32[]{:S(2)}) async-start(), calls=%async_computation.10 | async-start | bytes 2621440 | tf_op jit(solution)/shard_map/reduce_scatter | solution.py:84
  131.8 5.9 %slice-start = ((bf16[32,123904]{1,0:T(8,128)(2,1)}), bf16[32,24576]{1,0:T(8,128)(2,1)S(1)}, s32[]{:S(2)}) async-start(bf16[32,123904]{1,0:T(8,128)(2,1)} %reshape.418), calls=%async_computation.15 | async-start | bytes 3145728 | tf_op jit(solution)/shard_map/slice | solution.py:108
  143.2 5.7 %copy-start.3 = (bf16[32,32768]{1,0:T(8,128)(2,1)S(1)}, bf16[32,32768]{1,0:T(8,128)(2,1)}, u32[]{:S(2)}) copy-start(bf16[32,32768]{1,0:T(8,128)(2,1)} %get-tuple-element.35) | copy-start | bytes 6291460
  147.9 5.7 %copy-start.13 = (bf16[512,256]{0,1:T(8,128)(2,1)}, bf16[512,256]{0,1:T(8,128)(2,1)S(1)}, u32[]{:S(2)}) copy-start(bf16[512,256]{0,1:T(8,128)(2,1)S(1)} %copy.75) | copy-start | bytes 786436
  148.9 2.4 copy-start.21
  148.9 2.4 copy-start.19
  153.6 2.0 copy-start.32
  155.6 0.7 copy-start.17
  188.7 18.3 %all-to-all-start.1 = ((bf16[4,128,1024]{2,1,0:T(8,128)(2,1)}), bf16[4,128,1024]{2,1,0:T(8,128)(2,1)}, u32[]{:S(2)}, u32[]{:S(2)}) async-start(bf16[4,128,1024]{2,1,0:T(8,128)(2,1)} %stack.63), calls=%async_computation.2 | async-start | bytes 2097152 | tf_op jit(solution)/shard_map/all_to_all | solution.py:17
  193.3 50.9 %reduce-scatter.7.cloned.1.call-start = ((), (), s32[]{:S(2)}) async-start(), calls=%async_computation.11 | async-start | bytes 2621440 | tf_op jit(solution)/shard_map/reduce_scatter | solution.py:84
  194.1 4.4 copy-start.2
  207.0 4.7 copy-start.7
  211.7 2.6 copy-start.34
  214.3 31.4 %copy-start.5 = (f32[1,128,1024]{2,1,0:T(8,128)S(1)}, f32[1,128,1024]{2,1,0:T(8,128)}, u32[]{:S(2)}) copy-start(f32[1,128,1024]{2,1,0:T(8,128)} %param.12) | copy-start | bytes 1572868
  214.3 85.8 %reduce-scatter.9.cloned.1.call-start = ((), (), s32[]{:S(2)}) async-start(), calls=%async_computation.12 | async-start | bytes 2621440 | tf_op jit(solution)/shard_map/reduce_scatter | solution.py:84
  247.1 17.2 %copy-start.8 = (bf16[1024,1024]{1,0:T(8,128)(2,1)S(1)}, bf16[1024,1024]{1,0:T(8,128)(2,1)}, u32[]{:S(2)}) copy-start(bf16[1024,1024]{1,0:T(8,128)(2,1)} %reshape.393) | copy-start | bytes 6291460
  247.1 17.2 %copy-start.35 = (f32[512,1024]{1,0:T(8,128)S(1)}, f32[512,1024]{1,0:T(8,128)}, u32[]{:S(2)}) copy-start(f32[512,1024]{1,0:T(8,128)} %get-tuple-element.49) | copy-start | bytes 6291460
  264.3 2.2 copy-start.15
  264.3 3.1 copy-start.6
  266.4 1.0 copy-start.36
  270.1 1.2 copy-start.16
  302.9 18.3 %all-to-all-start.3 = ((bf16[4,128,1024]{2,1,0:T(8,128)(2,1)}), bf16[4,128,1024]{2,1,0:T(8,128)(2,1)}, u32[]{:S(2)}, u32[]{:S(2)}) async-start(bf16[4,128,1024]{2,1,0:T(8,128)(2,1)} %stack.65), calls=%async_computation.6 | async-start | bytes 2097152 | tf_op jit(solution)/shard_map/all_to_all | solution.py:17
  321.2 60.6 %all-to-all-start.5 = ((bf16[32,8,8192]{2,1,0:T(8,128)(2,1)}), bf16[32,8,8192]{2,1,0:T(8,128)(2,1)}, u32[]{:S(2)}, u32[]{:S(2)}) async-start(bf16[32,8,8192]{2,1,0:T(8,128)(2,1)} %pad_maximum_fusion), calls=%async_computation.9 | async-start | bytes 8388608 | tf_op jit(solution)/shard_map/all_to_all | solution.py:180
  330.6 1.9 copy-start.14
  332.5 2.9 copy-start.20
  332.5 3.6 copy-start.33
  336.1 1.1 copy-start.23
  337.3 7.4 %copy-start.22 = (bf16[512,256]{0,1:T(8,128)(2,1)S(1)}, bf16[512,256]{0,1:T(8,128)(2,1)}, u32[]{:S(2)}) copy-start(bf16[512,256]{0,1:T(8,128)(2,1)} %copy-done.21) | copy-start | bytes 786436
  344.7 8.9 %copy-start.28 = (bf16[4,64,512]{2,1,0:T(8,128)(2,1)}, bf16[4,64,512]{2,1,0:T(8,128)(2,1)S(1)}, u32[]{:S(2)}) copy-start(bf16[4,64,512]{2,1,0:T(8,128)(2,1)S(1)} %fusion.29) | copy-start | bytes 786436
  344.7 8.9 %copy-start.12 = (bf16[4,128,1152]{2,1,0:T(8,128)(2,1)S(1)}, bf16[4,128,1152]{2,1,0:T(8,128)(2,1)}, u32[]{:S(2)}) copy-start(bf16[4,128,1152]{2,1,0:T(8,128)(2,1)} %copy.72) | copy-start | bytes 3538948
  353.5 2.2 copy-start.30
  357.6 2.9 copy-start.18
  381.8 8.8 %copy-start.11 = (bf16[1024,768]{1,0:T(8,128)(2,1)S(1)}, bf16[1024,768]{1,0:T(8,128)(2,1)}, u32[]{:S(2)}) copy-start(bf16[1024,768]{1,0:T(8,128)(2,1)} %reshape.383) | copy-start | bytes 4718596
  381.8 8.8 %copy-start.29 = (bf16[4,64,512]{2,1,0:T(8,128)(2,1)S(1)}, bf16[4,64,512]{2,1,0:T(8,128)(2,1)}, u32[]{:S(2)}) copy-start(bf16[4,64,512]{2,1,0:T(8,128)(2,1)} %copy-done.28) | copy-start | bytes 786436
  381.8 8.8 %copy-start.31 = (bf16[1,512,4,64]{1,3,2,0:T(8,128)(2,1)S(1)}, bf16[1,512,4,64]{1,3,2,0:T(8,128)(2,1)}, u32[]{:S(2)}) copy-start(bf16[1,512,4,64]{1,3,2,0:T(8,128)(2,1)} %copy-done.30) | copy-start | bytes 786436
  381.8 53.5 %all-to-all-start.4 = ((bf16[32,8,7296]{2,1,0:T(8,128)(2,1)}), bf16[32,8,7296]{2,1,0:T(8,128)(2,1)}, u32[]{:S(2)}, u32[]{:S(2)}) async-start(bf16[32,8,7296]{2,1,0:T(8,128)(2,1)} %bitcast.101), calls=%async_computation.8 | async-start | bytes 7471104 | tf_op jit(solution)/shard_map/all_to_all | solution.py:239
  390.3 88.4 %reduce-scatter.11.cloned.1.call-start = ((), (), s32[]{:S(2)}) async-start(), calls=%async_computation.13 | async-start | bytes 2621440 | tf_op jit(solution)/shard_map/reduce_scatter | solution.py:84
  458.6 6.1 %copy-start.4 = (f32[4,123904]{1,0:T(4,128)}, f32[4,123904]{1,0:T(4,128)S(1)}, u32[]{:S(2)}) copy-start(f32[4,123904]{1,0:T(4,128)S(1)} %reshape.420) | copy-start | bytes 5947396
  469.2 4.5 copy-start.10
  469.2 11.5 %copy-start.1 = (bf16[1,128,1024]{2,1,0:T(8,128)(2,1)S(1)}, bf16[1,128,1024]{2,1,0:T(8,128)(2,1)}, u32[]{:S(2)}) copy-start(bf16[1,128,1024]{2,1,0:T(8,128)(2,1)} %param.16) | copy-start | bytes 786436
Sparse Core Ops, SparseCore 0:
  16.3 106.3 all-gather.3
  159.3 26.6 reduce-scatter.4
  214.5 29.6 reduce-scatter.6
  270.3 29.8 reduce-scatter.8
  393.4 61.6 reduce-scatter.10
